TPU v7x, 32 devices: a whole 2x2x4 slice. The times are simulated.
32 devices in a mesh: dp: 8 (over y, x, core), tensor: 4 (over z).
Axes of the slice: x: 2, y: 2, z: 4, core: 2. Of those that a mesh axis runs over, the one named last changes fastest.
Arguments:
- inputs: bfloat16 [6144, 2048], P('dp', 'tensor'), may hold values from -6 to 6
- labels: int32 [6144], P('dp'), may hold values from 0 to 1
- cotangent: bfloat16 [6144, 2048], P('dp', 'tensor'), may hold values from -6 to 6
- gate_weight: bfloat16 [2048, 2], P('tensor'), may hold values from -0.125 to 0.125
- weight_in: bfloat16 [3, 2048, 4096], P(None, None, 'tensor'), may hold values from -0.125 to 0.125
- weight_out: bfloat16 [3, 4096, 2048], P(None, 'tensor'), may hold values from -0.09375 to 0.09375
Outputs:
- input_grad: float32 [6144, 2048], P('dp', 'tensor')
- gate_grad: float32 [2048, 2], P('tensor')
- weight_in_grad: float32 [3, 2048, 4096], P(None, 'dp', 'tensor')
- weight_out_grad: float32 [3, 4096, 2048], P(None, 'tensor', 'dp')
All inputs are finite; a program needn't handle non-finite values.
Results may differ from a plain program's by a relative error of at most 0.0075.
Values may be sent and summed in bfloat16 or wider, within the bound.
A program may use at most 192 MiB of HBM per device.

v0:
```python
import jax
import jax.numpy as jnp
from jax import lax
from jax.sharding import PartitionSpec as P


def expert_grads(x_full, hidden_grad, active, share, cot_float):
    contract_rows = (((0,), (0,)), ((), ()))
    out_grad = (share * cot_float).astype(jnp.bfloat16)
    grad_one = lax.dot_general(
        x_full, hidden_grad, contract_rows, preferred_element_type=jnp.float32
    )
    grad_two = lax.dot_general(active, out_grad, contract_rows, preferred_element_type=jnp.float32)
    return (grad_one, grad_two)


def shards(inputs, labels, cotangent, gate_weight, weight_in, weight_out):
    contract_cols = (((1,), (1,)), ((), ()))
    num_tasks = gate_weight.shape[1]
    num_experts = weight_in.shape[0]
    x_full, cot_full = (
        lax.all_gather(inputs, "tensor", axis=1, tiled=True),
        lax.all_gather(cotangent, "tensor", axis=1, tiled=True),
    )
    logits = lax.psum(jnp.dot(inputs, gate_weight, preferred_element_type=jnp.float32), "tensor")
    picked = (labels[:, None] == jnp.arange(num_tasks, dtype=jnp.int32)[None, :]).astype(
        jnp.float32
    )
    task_gate = jax.nn.sigmoid(jnp.sum(logits * picked, axis=1))
    mixing = jnp.concatenate([(1.0 - task_gate)[:, None], task_gate[:, None] * picked], axis=1)
    cot_float = cot_full.astype(jnp.float32)
    scores = []
    actives = []
    hidden_grads = []
    grads_in = []
    grads_out = []
    partial_input = None
    for expert in range(num_experts):
        hidden = jnp.dot(x_full, weight_in[expert], preferred_element_type=jnp.float32)
        sigma = jax.nn.sigmoid(hidden)
        active = (hidden * sigma).astype(jnp.bfloat16)
        back_grad = lax.dot_general(
            cot_full, weight_out[expert], contract_cols, preferred_element_type=jnp.float32
        )
        scores.append(jnp.sum(active.astype(jnp.float32) * back_grad, axis=1))
        share = mixing[:, expert : expert + 1]
        hidden_grad = (share * back_grad * sigma * (1.0 + hidden * (1.0 - sigma))).astype(
            jnp.bfloat16
        )
        term = lax.dot_general(
            hidden_grad, weight_in[expert], contract_cols, preferred_element_type=jnp.float32
        )
        partial_input = term if partial_input is None else partial_input + term
        actives.append(active)
        hidden_grads.append(hidden_grad)
        grad_one, grad_two = expert_grads(x_full, hidden_grad, active, share, cot_float)
        grads_in.append(grad_one)
        grads_out.append(grad_two)
    score = lax.psum(jnp.stack(scores, axis=1), "tensor")
    own = jnp.sum(score[:, 1:] * picked, axis=1) - score[:, 0]
    slope = task_gate * (1.0 - task_gate) * own
    slope_rows = slope[:, None] * picked
    input_grad = lax.psum_scatter(partial_input, "tensor", scatter_dimension=1, tiled=True)
    input_grad = input_grad + jnp.dot(
        slope_rows, gate_weight.astype(jnp.float32).T, precision=lax.Precision.HIGHEST
    )
    gate_part = jnp.dot(inputs.astype(jnp.float32).T, slope_rows, precision=lax.Precision.HIGHEST)
    gate_grad = lax.psum(gate_part, "dp")
    weight_in_grad, weight_out_grad = (
        lax.psum_scatter(jnp.stack(grads_in), "dp", scatter_dimension=1, tiled=True),
        lax.psum_scatter(jnp.stack(grads_out), "dp", scatter_dimension=2, tiled=True),
    )
    return (input_grad, gate_grad, weight_in_grad, weight_out_grad)


def solution(mesh):
    in_specs = (
        P("dp", "tensor"),
        P("dp"),
        P("dp", "tensor"),
        P("tensor", None),
        P(None, None, "tensor"),
        P(None, "tensor", None),
    )
    out_specs = (
        P("dp", "tensor"),
        P("tensor", None),
        P(None, "dp", "tensor"),
        P(None, "tensor", "dp"),
    )
    return jax.shard_map(shards, mesh=mesh, in_specs=in_specs, out_specs=out_specs, check_vma=False)
```

profile of v0, /device:TPU:0, one launch (start us, length us, event | category | flops | bytes accessed | tf_op | source)
XLA Modules:
  0.0 653.9 jit_solution(352505402512204216)
XLA Ops:
  7.2 0.0 copy-start
  7.2 0.0 all-gather.5.cloned.1.call-start
  7.2 0.7 all-gather.5.cloned.1.call-update
  7.9 0.0 all-gather.3.cloned.1.call-start
  8.0 0.7 all-gather.3.cloned.1.call-update
  8.7 0.0 reduce-scatter.4.cloned.1.call-start
  8.7 0.0 copy-done
  8.7 1.4 fusion.52
  10.1 65.6 %all-gather.5.cloned.1.call-done = bf16[768,2048]{1,0:T(8,128)(2,1)} async-done(((bf16[768,512]{1,0:T(8,128)(2,1)}), bf16[768,2048]{1,0:T(8,128)(2,1)}) %all-gather.5.cloned.1.call-update) | async-done | bytes 3145744 | tf_op jit(solution)/shard_map/all_gather | solution.py:22
  75.8 6.1 fusion.17
  81.9 57.6 %all-gather.3.cloned.1.call-done = bf16[768,2048]{1,0:T(8,128)(2,1)} async-done(((bf16[768,512]{1,0:T(8,128)(2,1)}), bf16[768,2048]{1,0:T(8,128)(2,1)}) %all-gather.3.cloned.1.call-update) | async-done | bytes 3145744 | tf_op jit(solution)/shard_map/all_gather | solution.py:23
  139.4 8.6 %multiply_reduce_fusion.2 = (f32[768]{0:T(1024)S(1)}, f32[768,1024]{1,0:T(8,128)}) fusion(f32[768,1024]{1,0:T(8,128)S(1)} %fusion.17, bf16[768,2048]{1,0:T(8,128)(2,1)} %all-gather.3.cloned.1.call-done, bf16[3,1024,2048]{2,1,0:T(8,128)(2,1)} %param.11), kind=kOutput, calls=%fused_computation.49 | convolution fusion | flops 3227516160 | bytes 13634560 | tf_op jit(solution)/shard_map/dot_general | solution.py:42
  148.0 0.0 copy-done.14
  148.1 0.0 copy-start.12
  148.1 5.3 fusion.11
  153.4 0.0 slice-done
  153.4 0.0 slice-done.1
  153.4 0.0 slice-done.2
  153.4 0.0 copy-done.12
  153.5 0.0 copy-start.2
  153.5 5.3 multiply_reduce_fusion.1
  158.8 5.7 fusion.5
  164.5 0.0 copy-start.3
  164.5 0.0 copy-start.11
  164.5 5.3 multiply_reduce_fusion
  169.9 16.4 %all-reduce = (f32[768,3]{0,1:T(4,128)S(1)}, f32[768,2]{0,1:T(2,128)S(1)}) all-reduce(f32[768,3]{0,1:T(4,128)S(1)} %pad_maximum_fusion.2, f32[768,2]{0,1:T(2,128)S(1)} %fusion.52), channel_id=1, replica_groups=mesh['dp'=8,'tensor'=4] {'tensor'}, use_global_device_ids=true, to_apply=%region_6.0 | all-reduce | flops 3840 | bytes 30720 | tf_op jit(solution)/shard_map/psum | solution.py:59
  186.2 0.0 copy-done.11
  186.3 0.0 slice-start.3
  186.3 0.0 slice-start.4
  186.3 6.0 multiply_convert_fusion.3
  192.4 0.0 copy-start.6
  192.4 0.0 copy-start.8
  192.4 0.0 slice-start.5
  192.4 8.7 %fusion.3 = f32[768,2048]{1,0:T(8,128)} fusion(bf16[768,1024]{1,0:T(8,128)(2,1)S(1)} %get-tuple-element.22, bf16[3,2048,1024]{2,1,0:T(8,128)(2,1)} %param.10), kind=kOutput, calls=%fused_computation.15 | convolution fusion | flops 3221225472 | bytes 12058624 | tf_op jit(solution)/shard_map/dot_general | solution.py:50
  201.1 0.0 copy-done.8
  201.1 5.4 fusion.9
  206.6 1.3 multiply_convert_fusion.5
  207.9 1.1 copy-done.10
  209.0 8.3 %add_add_fusion = f32[768,2048]{1,0:T(8,128)} fusion(f32[768,2048]{1,0:T(8,128)} %fusion.3, f32[768,2048]{1,0:T(8,128)} %fusion.9, bf16[768,1024]{1,0:T(8,128)(2,1)S(1)} %multiply_convert_fusion.5, bf16[3,2048,1024]{2,1,0:T(8,128)(2,1)S(1)} %bitcast.74), kind=kOutput, calls=%fused_computation.8 | convolution fusion | flops 3224371200 | bytes 24641536 | tf_op jit(solution)/shard_map/dot_general | solution.py:50
  217.3 0.0 reduce-scatter.4.cloned.1.call-update
  217.3 0.2 reduce-scatter.6.cloned.1.call-start
  217.5 0.0 copy-start.9
  217.5 6.1 convolution_bitcast_fusion.5
  223.6 0.0 copy-start.7
  223.6 3.5 convolution_bitcast_fusion.4
  227.2 3.6 convolution_bitcast_fusion.3
  230.8 9.0 %pad_maximum_fusion = f32[3,2048,1024]{1,2,0:T(8,128)} fusion(f32[1,2048,1024]{1,2,0:T(8,128)S(1)} %convolution_bitcast_fusion.3, f32[1,2048,1024]{1,2,0:T(8,128)S(1)} %convolution_bitcast_fusion.4, f32[1,2048,1024]{1,2,0:T(8,128)S(1)} %convolution_bitcast_fusion.5), kind=kLoop, calls=%fused_computation | loop fusion | flops 12582912 | bytes 50331648 | tf_op jit(solution)/shard_map/stack | solution.py:70
  239.7 0.0 reduce-scatter.6.cloned.1.call-update
  239.7 0.3 reduce-scatter.8.cloned.1.call-start
  240.0 0.0 copy-start.4
  240.0 0.0 copy-start.13
  240.0 6.7 %convolution_bitcast_fusion.1 = f32[1,1024,2048]{2,1,0:T(8,128)S(1)} fusion(bf16[768,2048]{1,0:T(8,128)(2,1)} %all-gather.3.cloned.1.call-done, f32[768]{0:T(1024)S(1)} %get-tuple-element.8, f32[768,1024]{1,0:T(8,128)} %copy-done.2), kind=kOutput, calls=%fused_computation.10 | convolution fusion | flops 3229876224 | bytes 14683136 | tf_op jit(solution)/shard_map/dot_general | solution.py:13
  246.7 3.7 convolution_bitcast_fusion
  250.4 3.7 convolution_bitcast_fusion.2
  254.2 8.7 %pad_maximum_fusion.1 = f32[3,1024,2048]{2,1,0:T(8,128)} fusion(f32[1,1024,2048]{2,1,0:T(8,128)S(1)} %convolution_bitcast_fusion, f32[1,1024,2048]{2,1,0:T(8,128)S(1)} %convolution_bitcast_fusion.1, f32[1,1024,2048]{2,1,0:T(8,128)S(1)} %convolution_bitcast_fusion.2), kind=kLoop, calls=%fused_computation.1 | loop fusion | flops 12582912 | bytes 50331648 | tf_op jit(solution)/shard_map/stack | solution.py:71
  262.9 0.0 reduce-scatter.8.cloned.1.call-update
  262.9 1.1 copy-done.1
  264.0 0.4 convolution_bitcast_fusion.6
  264.4 12.8 %psum.23 = f32[512,2]{0,1:T(2,128)} all-reduce(f32[512,2]{0,1:T(2,128)S(1)} %convolution_bitcast_fusion.6), channel_id=1, replica_groups=mesh['dp'=8,'tensor'=4] {'dp'}, use_global_device_ids=true, to_apply=%region_8.0 | all-reduce | flops 1024 | bytes 8192 | tf_op jit(solution)/shard_map/psum | solution.py:68
  277.2 49.9 %reduce-scatter.4.cloned.1.call-done = f32[768,512]{1,0:T(8,128)} async-done(((f32[768,2048]{1,0:T(8,128)}), f32[768,512]{1,0:T(8,128)}) %reduce-scatter.4.cloned.1.call-update) | async-done | bytes 1572880 | tf_op jit(solution)/shard_map/reduce_scatter | solution.py:63
  327.1 3.4 convolution_add_fusion
  330.5 156.6 %reduce-scatter.6.cloned.1.call-done = f32[3,256,1024]{1,2,0:T(8,128)} async-done(((f32[3,2048,1024]{1,2,0:T(8,128)}), f32[3,256,1024]{1,2,0:T(8,128)}) %reduce-scatter.6.cloned.1.call-update) | async-done | bytes 3145744 | tf_op jit(solution)/shard_map/reduce_scatter | solution.py:70
  487.1 3.5 copy.10
  490.6 156.5 %reduce-scatter.8.cloned.1.call-done = f32[3,1024,256]{2,1,0:T(8,128)} async-done(((f32[3,1024,2048]{2,1,0:T(8,128)}), f32[3,1024,256]{2,1,0:T(8,128)}) %reduce-scatter.8.cloned.1.call-update) | async-done | bytes 3145744 | tf_op jit(solution)/shard_map/reduce_scatter | solution.py:71
  (31 shorter events, 0.1 us)
Async XLA Ops:
  7.2 1.5 copy-start
  7.2 68.6 %all-gather.5.cloned.1.call-start = ((), (), s32[]{:S(2)}) async-start(), calls=%async_computation.4 | async-start | bytes 3932160 | tf_op jit(solution)/shard_map/all_gather | solution.py:22
  7.9 131.5 %all-gather.3.cloned.1.call-start = ((), (), s32[]{:S(2)}) async-start(), calls=%async_computation.3 | async-start | bytes 3932160 | tf_op jit(solution)/shard_map/all_gather | solution.py:23
  8.7 318.4 %reduce-scatter.4.cloned.1.call-start = ((), (), s32[]{:S(2)}) async-start(), calls=%async_computation.5 | async-start | bytes 7864320 | tf_op jit(solution)/shard_map/reduce_scatter | solution.py:63
  139.4 8.6 %copy-start.14 = (bf16[768,2048]{1,0:T(8,128)(2,1)S(1)}, bf16[768,2048]{1,0:T(8,128)(2,1)}, u32[]{:S(2)}) copy-start(bf16[768,2048]{1,0:T(8,128)(2,1)} %all-gather.5.cloned.1.call-done) | copy-start | bytes 9437188
  139.4 14.0 %slice-start = ((s8[12582912]{0:T(1024)(128)(4,1)}), s8[4194304]{0:T(1024)(128)(4,1)S(1)}, s32[]{:S(2)}) async-start(s8[12582912]{0:T(1024)(128)(4,1)} %bitcast.71), calls=%async_computation.8 | async-start | bytes 8388608
  139.4 14.0 %slice-start.1 = ((s8[12582912]{0:T(1024)(128)(4,1)}), s8[4194304]{0:T(1024)(128)(4,1)S(1)}, s32[]{:S(2)}) async-start(s8[12582912]{0:T(1024)(128)(4,1)} %bitcast.71), calls=%async_computation.9 | async-start | bytes 8388608
  148.0 5.4 slice-start.2
  148.1 5.4 copy-start.12
  153.5 5.3 copy-start.2
  164.5 5.4 copy-start.3
  164.5 21.8 %copy-start.11 = (s32[768]{0:T(1024)S(1)}, s32[768]{0:T(1024)}, u32[]{:S(2)}) copy-start(s32[768]{0:T(1024)} %param.7) | copy-start | bytes 9220
  186.3 14.8 %slice-start.3 = ((s8[12582912]{0:T(1024)(128)(4,1)}), s8[4194304]{0:T(1024)(128)(4,1)S(1)}, s32[]{:S(2)}) async-start(s8[12582912]{0:T(1024)(128)(4,1)} %bitcast.73), calls=%async_computation.11 | async-start | bytes 8388608
  186.3 14.8 %slice-start.4 = ((s8[12582912]{0:T(1024)(128)(4,1)}), s8[4194304]{0:T(1024)(128)(4,1)S(1)}, s32[]{:S(2)}) async-start(s8[12582912]{0:T(1024)(128)(4,1)} %bitcast.73), calls=%async_computation.12 | async-start | bytes 8388608
  192.4 8.7 %copy-start.6 = (bf16[768,1024]{1,0:T(8,128)(2,1)}, bf16[768,1024]{1,0:T(8,128)(2,1)S(1)}, u32[]{:S(2)}) copy-start(bf16[768,1024]{1,0:T(8,128)(2,1)S(1)} %get-tuple-element.22) | copy-start | bytes 4718596
  192.4 8.7 %copy-start.8 = (bf16[768,1024]{1,0:T(8,128)(2,1)}, bf16[768,1024]{1,0:T(8,128)(2,1)S(1)}, u32[]{:S(2)}) copy-start(bf16[768,1024]{1,0:T(8,128)(2,1)S(1)} %get-tuple-element.23) | copy-start | bytes 4718596
  192.4 8.7 %slice-start.5 = ((s8[12582912]{0:T(1024)(128)(4,1)}), s8[4194304]{0:T(1024)(128)(4,1)S(1)}, s32[]{:S(2)}) async-start(s8[12582912]{0:T(1024)(128)(4,1)} %bitcast.73), calls=%async_computation.13 | async-start | bytes 8388608
  201.1 5.4 copy-start.5
  207.8 1.1 copy-start.10
  217.3 269.8 %reduce-scatter.6.cloned.1.call-start = ((), (), s32[]{:S(2)}) async-start(), calls=%async_computation.6 | async-start | bytes 28311552 | tf_op jit(solution)/shard_map/reduce_scatter | solution.py:70
  217.5 6.1 copy-start.9
  217.5 6.1 copy-start.15
  223.6 3.6 copy-start.7
  239.7 407.4 %reduce-scatter.8.cloned.1.call-start = ((), (), s32[]{:S(2)}) async-start(), calls=%async_computation.7 | async-start | bytes 28311552 | tf_op jit(solution)/shard_map/reduce_scatter | solution.py:71
  240.0 6.7 %copy-start.4 = (f32[768,1024]{1,0:T(8,128)S(1)}, f32[768,1024]{1,0:T(8,128)}, u32[]{:S(2)}) copy-start(f32[768,1024]{1,0:T(8,128)} %copy-done.3) | copy-start | bytes 9437188
  240.0 6.7 %copy-start.13 = (bf16[768,2048]{1,0:T(8,128)(2,1)S(1)}, bf16[768,2048]{1,0:T(8,128)(2,1)}, u32[]{:S(2)}) copy-start(bf16[768,2048]{1,0:T(8,128)(2,1)} %all-gather.3.cloned.1.call-done) | copy-start | bytes 9437188
  262.9 1.1 copy-start.1
Sparse Core Ops, SparseCore 0:
  9.6 66.1 all-gather.4
  77.3 62.0 all-gather.2
  217.4 109.6 reduce-scatter.3
  330.5 156.5 reduce-scatter.5
  491.1 155.9 reduce-scatter.7
where the time goes:
time: 661 us; the launch traced here: 654 us
  waiting for transfers between devices  488 us (74%)
  matrix products  91.3 us (14%)
  blocking collectives  29.1 us (4%)
  other arithmetic  25 us (4%)
  between operations  14.4 us (2%)
    reduce_scatter x1, waiting for transfers between devices, shards(): lax.psum_scatter(jnp.stack(grads_in), 'dp', scatter_dimension=1, tiled=True)  157 us
    reduce_scatter x1, waiting for transfers between devices, shards(): lax.psum_scatter(jnp.stack(grads_out), 'dp', scatter_dimension=2, tiled=T...  157 us
    all_gather x1, waiting for transfers between devices, shards(): lax.all_gather(inputs, 'tensor', axis=1, tiled=True)  65.6 us
    all_gather x1, waiting for transfers between devices, shards(): lax.all_gather(cotangent, 'tensor', axis=1, tiled=True)  57.6 us
    reduce_scatter x1, waiting for transfers between devices, shards(): lax.psum_scatter(partial_input, 'tensor', scatter_dimension=1, tiled=True)  49.9 us
    dot_general x3, matrix products, shards(): lax.dot_general(hidden_grad, weight_in[expert], contract_cols, preferred_...  22.4 us
    dot_general x3, matrix products, shards(): lax.dot_general(cot_full, weight_out[expert], contract_cols, preferred_el...  19.2 us
    dot_general x3, matrix products, shards(): jnp.dot(x_full, weight_in[expert], preferred_element_type=jnp.float32)  17.1 us
  transfers between devices with their start and end apart: 5, of which 5 were waited for; matrix products, arithmetic and copies ran while one was open for 9% of the time, Pallas kernels for 0%

commit v1 on v0

--- a/solution.py
+++ b/solution.py
@@ -2,6 +2,23 @@
 import jax.numpy as jnp
 from jax import lax
 from jax.sharding import PartitionSpec as P
+
+
+def joined_along(parts, dim):
+    parts = jnp.moveaxis(parts, 0, dim)
+    dims = parts.shape
+    return parts.reshape(*dims[:dim], dims[dim] * dims[dim + 1], *dims[dim + 2 :])
+
+
+def collect(array, axis, dim):
+    size = lax.axis_size(axis)
+    right = [(i, (i + 1) % size) for i in range(size)]
+    blocks = [array]
+    while len(blocks) < size:
+        blocks.append(lax.ppermute(blocks[-1], axis, right))
+    position = lax.axis_index(axis)
+    blocks = jnp.stack(blocks)[(position - jnp.arange(size)) % size]
+    return joined_along(blocks, dim)
 
 
 def expert_grads(x_full, hidden_grad, active, share, cot_float):
@@ -20,7 +37,7 @@
     num_experts = weight_in.shape[0]
     x_full, cot_full = (
         lax.all_gather(inputs, "tensor", axis=1, tiled=True),
-        lax.all_gather(cotangent, "tensor", axis=1, tiled=True),
+        collect(cotangent, "tensor", 1),
     )
     logits = lax.psum(jnp.dot(inputs, gate_weight, preferred_element_type=jnp.float32), "tensor")
     picked = (labels[:, None] == jnp.arange(num_tasks, dtype=jnp.int32)[None, :]).astype(

time: 661 us -> 654 us (0.989)
  waiting for transfers between devices: 488 us -> 445 us
  starting transfers between devices: 0.58 us -> 25.4 us
  local copies, waits for them, and re-layouts: 5.88 us -> 13.8 us
    ppermute x0 -> x3, waiting for transfers between devices: none -> 81.1 us  [collect(): blocks.append(lax.ppermute(blocks[-1], axis, right))]
    all_gather x1, waiting for transfers between devices: 65.6 us -> 0.01 us  [shards(): lax.all_gather(inputs, 'tensor', axis=1, tiled=True)]
    all_gather x1 -> x0, waiting for transfers between devices: 57.6 us -> none  [shards(): lax.all_gather(cotangent, 'tensor', axis=1, tiled=True)]
    ppermute x0 -> x3, starting transfers between devices: none -> 24.8 us  [collect(): blocks.append(lax.ppermute(blocks[-1], axis, right))]
  transfers between devices with their start and end apart: 5 -> 7, of which waited for: 5 -> 6; matrix products, arithmetic and copies ran while one was open for 9% -> 10% of each run, Pallas kernels for 0% -> 0%
where the time goes in v1:
time: 654 us; the launch traced here: 646 us
  waiting for transfers between devices  445 us (68%)
  matrix products  90.3 us (14%)
  blocking collectives  29.8 us (5%)
  other arithmetic  26.7 us (4%)
  starting transfers between devices  25.4 us (4%)
  between operations  14.4 us (2%)
  local copies, waits for them, and re-layouts  13.8 us (2%)
    reduce_scatter x1, waiting for transfers between devices, shards(): lax.psum_scatter(jnp.stack(grads_in), 'dp', scatter_dimension=1, tiled=True)  157 us
    reduce_scatter x1, waiting for transfers between devices, shards(): lax.psum_scatter(jnp.stack(grads_out), 'dp', scatter_dimension=2, tiled=T...  157 us
    ppermute x3, waiting for transfers between devices, collect(): blocks.append(lax.ppermute(blocks[-1], axis, right))  81.1 us
    reduce_scatter x1, waiting for transfers between devices, shards(): lax.psum_scatter(partial_input, 'tensor', scatter_dimension=1, tiled=True)  50 us
    ppermute x3, starting transfers between devices, collect(): blocks.append(lax.ppermute(blocks[-1], axis, right))  24.8 us
    dot_general x3, matrix products, shards(): lax.dot_general(hidden_grad, weight_in[expert], contract_cols, preferred_...  22.2 us
    dot_general x3, matrix products, shards(): lax.dot_general(cot_full, weight_out[expert], contract_cols, preferred_el...  18.6 us
    dot_general x3, matrix products, shards(): jnp.dot(x_full, weight_in[expert], preferred_element_type=jnp.float32)  17.3 us
  transfers between devices with their start and end apart: 7, of which 6 were waited for; matrix products, arithmetic and copies ran while one was open for 10% of the time, Pallas kernels for 0%

profile of v1, /device:TPU:0, one launch (start us, length us, event | category | flops | bytes accessed | tf_op | source)
XLA Modules:
  0.0 645.5 jit_solution(8803901157916880136)
XLA Ops:
  7.2 0.0 copy-start
  7.2 0.0 all-gather.2.cloned.1.call-start
  7.2 0.7 all-gather.2.cloned.1.call-update
  7.9 0.0 reduce-scatter.4.cloned.1.call-start
  8.0 3.1 collective-permute-start
  11.1 26.7 %collective-permute-done = bf16[768,512]{1,0:T(8,128)(2,1)S(1)} collective-permute-done((bf16[768,512]{1,0:T(8,128)(2,1)}, bf16[768,512]{1,0:T(8,128)(2,1)S(1)}, u32[]{:S(2)}, u32[]{:S(2)}) %collective-permute-start) | collective-permute-done | bytes 786464 | tf_op jit(solution)/shard_map/ppermute | solution.py:18
  37.8 6.9 %collective-permute-start.1 = (bf16[768,512]{1,0:T(8,128)(2,1)S(1)}, bf16[768,512]{1,0:T(8,128)(2,1)S(1)}, u32[]{:S(2)}, u32[]{:S(2)}) collective-permute-start(bf16[768,512]{1,0:T(8,128)(2,1)S(1)} %collective-permute-done), channel_id=1, source_target_pairs={{0,1},{1,2},{2,3},{3,0},{4,5},{5,6},{6,7},{7,4},{8,9},{9,10},{10,1... | collective-permute-start | bytes 2359304 | tf_op jit(solution)/shard_map/ppermute | solution.py:18
  44.7 38.8 %collective-permute-done.1 = bf16[768,512]{1,0:T(8,128)(2,1)S(1)} collective-permute-done((bf16[768,512]{1,0:T(8,128)(2,1)S(1)}, bf16[768,512]{1,0:T(8,128)(2,1)S(1)}, u32[]{:S(2)}, u32[]{:S(2)}) %collective-permute-start.1) | collective-permute-done | bytes 786464 | tf_op jit(solution)/shard_map/ppermute | solution.py:18
  83.5 14.8 %collective-permute-start.2 = (bf16[768,512]{1,0:T(8,128)(2,1)S(1)}, bf16[768,512]{1,0:T(8,128)(2,1)S(1)}, u32[]{:S(2)}, u32[]{:S(2)}) collective-permute-start(bf16[768,512]{1,0:T(8,128)(2,1)S(1)} %collective-permute-done.1), channel_id=1, source_target_pairs={{0,1},{1,2},{2,3},{3,0},{4,5},{5,6},{6,7},{7,4},{8,9},{9,10},{10,1... | collective-permute-start | bytes 2359304 | tf_op jit(solution)/shard_map/ppermute | solution.py:18
  98.3 1.4 fusion.54
  99.7 15.7 %collective-permute-done.2 = bf16[768,512]{1,0:T(8,128)(2,1)S(1)} collective-permute-done((bf16[768,512]{1,0:T(8,128)(2,1)S(1)}, bf16[768,512]{1,0:T(8,128)(2,1)S(1)}, u32[]{:S(2)}, u32[]{:S(2)}) %collective-permute-start.2) | collective-permute-done | bytes 786464 | tf_op jit(solution)/shard_map/ppermute | solution.py:18
  115.4 0.0 copy-done.13
  115.4 0.9 copy-done.15
  116.3 2.0 pad_maximum_fusion.2
  118.3 2.4 gather_fusion
  120.8 4.6 copy.12
  125.4 6.3 fusion.17
  131.7 0.0 slice-start
  131.7 0.0 slice-start.1
  131.7 7.8 %multiply_reduce_fusion.2 = (f32[768]{0:T(1024)S(1)}, f32[768,1024]{1,0:T(8,128)}) fusion(f32[768,1024]{1,0:T(8,128)S(1)} %fusion.17, bf16[768,2048]{0,1:T(8,128)(2,1)S(1)} %bitcast.81, bf16[3,1024,2048]{2,1,0:T(8,128)(2,1)} %param.11), kind=kOutput, calls=%fused_computation.51 | convolution fusion | flops 3227516160 | bytes 13634560 | tf_op jit(solution)/shard_map/dot_general | solution.py:59
  139.5 5.3 fusion.11
  144.9 5.4 multiply_reduce_fusion.1
  150.3 5.7 fusion.5
  156.0 0.0 copy-start.3
  156.0 0.0 copy-start.16
  156.0 5.4 multiply_reduce_fusion
  161.5 17.0 %all-reduce = (f32[768,3]{0,1:T(4,128)S(1)}, f32[768,2]{0,1:T(2,128)S(1)}) all-reduce(f32[768,3]{0,1:T(4,128)S(1)} %pad_maximum_fusion.3, f32[768,2]{0,1:T(2,128)S(1)} %fusion.54), channel_id=1, replica_groups=mesh['dp'=8,'tensor'=4] {'tensor'}, use_global_device_ids=true, to_apply=%region_6.7 | all-reduce | flops 3840 | bytes 30720 | tf_op jit(solution)/shard_map/psum | solution.py:76
  178.6 0.0 slice-start.3
  178.6 0.0 slice-start.4
  178.6 6.0 multiply_convert_fusion.3
  184.6 0.0 copy-start.8
  184.6 0.0 copy-start.10
  184.6 0.0 slice-start.5
  184.6 8.7 %fusion.3 = f32[768,2048]{1,0:T(8,128)} fusion(bf16[768,1024]{1,0:T(8,128)(2,1)S(1)} %get-tuple-element.30, bf16[3,2048,1024]{2,1,0:T(8,128)(2,1)} %param.10), kind=kOutput, calls=%fused_computation.16 | convolution fusion | flops 3221225472 | bytes 12058624 | tf_op jit(solution)/shard_map/dot_general | solution.py:67
  193.3 0.0 copy-done.8
  193.3 0.0 slice-done.3
  193.4 5.4 fusion.9
  198.7 1.3 multiply_convert_fusion.5
  200.0 1.1 copy-done.12
  201.2 8.1 %add_add_fusion = f32[768,2048]{1,0:T(8,128)} fusion(f32[768,2048]{1,0:T(8,128)} %fusion.3, f32[768,2048]{1,0:T(8,128)} %fusion.9, bf16[768,1024]{1,0:T(8,128)(2,1)S(1)} %multiply_convert_fusion.5, bf16[3,2048,1024]{2,1,0:T(8,128)(2,1)S(1)} %bitcast.93), kind=kOutput, calls=%fused_computation.9 | convolution fusion | flops 3224371200 | bytes 24641536 | tf_op jit(solution)/shard_map/dot_general | solution.py:67
  209.3 0.0 reduce-scatter.4.cloned.1.call-update
  209.3 0.2 reduce-scatter.6.cloned.1.call-start
  209.6 6.1 convolution_bitcast_fusion.5
  215.7 0.0 copy-start.9
  215.7 3.5 convolution_bitcast_fusion.4
  219.2 3.6 convolution_bitcast_fusion.3
  222.8 8.7 %pad_maximum_fusion = f32[3,2048,1024]{1,2,0:T(8,128)} fusion(f32[1,2048,1024]{1,2,0:T(8,128)S(1)} %convolution_bitcast_fusion.3, f32[1,2048,1024]{1,2,0:T(8,128)S(1)} %convolution_bitcast_fusion.4, f32[1,2048,1024]{1,2,0:T(8,128)S(1)} %convolution_bitcast_fusion.5), kind=kLoop, calls=%fused_computation.1 | loop fusion | flops 12582912 | bytes 50331648 | tf_op jit(solution)/shard_map/stack | solution.py:87
  231.5 0.0 reduce-scatter.6.cloned.1.call-update
  231.5 0.3 reduce-scatter.8.cloned.1.call-start
  231.8 0.0 copy-start.4
  231.8 0.0 copy-start.7
  231.8 6.6 %convolution_bitcast_fusion.1 = f32[1,1024,2048]{2,1,0:T(8,128)S(1)} fusion(bf16[768,2048]{0,1:T(8,128)(2,1)} %bitcast.80, f32[768]{0:T(1024)S(1)} %get-tuple-element.16, f32[768,1024]{1,0:T(8,128)} %copy-done.2), kind=kOutput, calls=%fused_computation.11 | convolution fusion | flops 3229876224 | bytes 14683136 | tf_op jit(solution)/shard_map/dot_general | solution.py:30
  238.4 3.6 convolution_bitcast_fusion
  242.0 3.6 convolution_bitcast_fusion.2
  245.6 8.6 %pad_maximum_fusion.1 = f32[3,1024,2048]{2,1,0:T(8,128)} fusion(f32[1,1024,2048]{2,1,0:T(8,128)S(1)} %convolution_bitcast_fusion, f32[1,1024,2048]{2,1,0:T(8,128)S(1)} %convolution_bitcast_fusion.1, f32[1,1024,2048]{2,1,0:T(8,128)S(1)} %convolution_bitcast_fusion.2), kind=kLoop, calls=%fused_computation.2 | loop fusion | flops 12582912 | bytes 50331648 | tf_op jit(solution)/shard_map/stack | solution.py:88
  254.2 0.0 reduce-scatter.8.cloned.1.call-update
  254.3 1.1 copy-done.1
  255.4 0.4 convolution_bitcast_fusion.6
  255.8 12.8 %psum.23 = f32[512,2]{0,1:T(2,128)} all-reduce(f32[512,2]{0,1:T(2,128)S(1)} %convolution_bitcast_fusion.6), channel_id=1, replica_groups=mesh['dp'=8,'tensor'=4] {'dp'}, use_global_device_ids=true, to_apply=%region_8.9 | all-reduce | flops 1024 | bytes 8192 | tf_op jit(solution)/shard_map/psum | solution.py:85
  268.5 50.0 %reduce-scatter.4.cloned.1.call-done = f32[768,512]{1,0:T(8,128)} async-done(((f32[768,2048]{1,0:T(8,128)}), f32[768,512]{1,0:T(8,128)}) %reduce-scatter.4.cloned.1.call-update) | async-done | bytes 1572880 | tf_op jit(solution)/shard_map/reduce_scatter | solution.py:80
  318.5 3.4 convolution_add_fusion
  321.9 156.8 %reduce-scatter.6.cloned.1.call-done = f32[3,256,1024]{1,2,0:T(8,128)} async-done(((f32[3,2048,1024]{1,2,0:T(8,128)}), f32[3,256,1024]{1,2,0:T(8,128)}) %reduce-scatter.6.cloned.1.call-update) | async-done | bytes 3145744 | tf_op jit(solution)/shard_map/reduce_scatter | solution.py:87
  478.7 3.5 copy.13
  482.2 156.5 %reduce-scatter.8.cloned.1.call-done = f32[3,1024,256]{2,1,0:T(8,128)} async-done(((f32[3,1024,2048]{2,1,0:T(8,128)}), f32[3,1024,256]{2,1,0:T(8,128)}) %reduce-scatter.8.cloned.1.call-update) | async-done | bytes 3145744 | tf_op jit(solution)/shard_map/reduce_scatter | solution.py:88
  (45 shorter events, 0.2 us)
Async XLA Ops:
  7.2 91.1 %copy-start = (bf16[512,2]{0,1:T(2,128)(2,1)S(1)}, bf16[512,2]{0,1:T(2,128)(2,1)}, u32[]{:S(2)}) copy-start(bf16[512,2]{0,1:T(2,128)(2,1)} %param.9) | copy-start | bytes 6148
  7.2 118.2 %all-gather.2.cloned.1.call-start = ((), (), s32[]{:S(2)}) async-start(), calls=%async_computation.3 | async-start | bytes 3932160 | tf_op jit(solution)/shard_map/all_gather | solution.py:39
  7.9 310.6 %reduce-scatter.4.cloned.1.call-start = ((), (), s32[]{:S(2)}) async-start(), calls=%async_computation.4 | async-start | bytes 7864320 | tf_op jit(solution)/shard_map/reduce_scatter | solution.py:80
  8.0 29.8 %collective-permute-start = (bf16[768,512]{1,0:T(8,128)(2,1)}, bf16[768,512]{1,0:T(8,128)(2,1)S(1)}, u32[]{:S(2)}, u32[]{:S(2)}) collective-permute-start(bf16[768,512]{1,0:T(8,128)(2,1)} %param.8), channel_id=1, source_target_pairs={{0,1},{1,2},{2,3},{3,0},{4,5},{5,6},{6,7},{7,4},{8,9},{9,10},{10,1... | collective-permute-start | bytes 2359304 | tf_op jit(solution)/shard_map/ppermute | solution.py:18
  37.8 77.7 %copy-start.13 = (bf16[768,512]{1,0:T(8,128)(2,1)}, bf16[768,512]{1,0:T(8,128)(2,1)S(1)}, u32[]{:S(2)}) copy-start(bf16[768,512]{1,0:T(8,128)(2,1)S(1)} %collective-permute-done) | copy-start | bytes 2359300
  37.8 45.7 %collective-permute-start.1 = (bf16[768,512]{1,0:T(8,128)(2,1)S(1)}, bf16[768,512]{1,0:T(8,128)(2,1)S(1)}, u32[]{:S(2)}, u32[]{:S(2)}) collective-permute-start(bf16[768,512]{1,0:T(8,128)(2,1)S(1)} %collective-permute-done), channel_id=1, source_target_pairs={{0,1},{1,2},{2,3},{3,0},{4,5},{5,6},{6,7},{7,4},{8,9},{9,10},{10,1... | collective-permute-start | bytes 2359304 | tf_op jit(solution)/shard_map/ppermute | solution.py:18
  83.4 32.0 %copy-start.14 = (bf16[768,512]{1,0:T(8,128)(2,1)}, bf16[768,512]{1,0:T(8,128)(2,1)S(1)}, u32[]{:S(2)}) copy-start(bf16[768,512]{1,0:T(8,128)(2,1)S(1)} %collective-permute-done.1) | copy-start | bytes 2359300
  83.5 32.0 %collective-permute-start.2 = (bf16[768,512]{1,0:T(8,128)(2,1)S(1)}, bf16[768,512]{1,0:T(8,128)(2,1)S(1)}, u32[]{:S(2)}, u32[]{:S(2)}) collective-permute-start(bf16[768,512]{1,0:T(8,128)(2,1)S(1)} %collective-permute-done.1), channel_id=1, source_target_pairs={{0,1},{1,2},{2,3},{3,0},{4,5},{5,6},{6,7},{7,4},{8,9},{9,10},{10,1... | collective-permute-start | bytes 2359304 | tf_op jit(solution)/shard_map/ppermute | solution.py:18
  115.4 0.9 copy-start.15
  125.4 6.3 copy-start.6
  131.7 7.8 %copy-start.17 = (bf16[768,2048]{1,0:T(8,128)(2,1)S(1)}, bf16[768,2048]{1,0:T(8,128)(2,1)}, u32[]{:S(2)}) copy-start(bf16[768,2048]{1,0:T(8,128)(2,1)} %all-gather.2.cloned.1.call-done) | copy-start | bytes 9437188
  131.7 13.2 %slice-start = ((s8[12582912]{0:T(1024)(128)(4,1)}), s8[4194304]{0:T(1024)(128)(4,1)S(1)}, s32[]{:S(2)}) async-start(s8[12582912]{0:T(1024)(128)(4,1)} %bitcast.90), calls=%async_computation.7 | async-start | bytes 8388608
  131.7 13.2 %slice-start.1 = ((s8[12582912]{0:T(1024)(128)(4,1)}), s8[4194304]{0:T(1024)(128)(4,1)S(1)}, s32[]{:S(2)}) async-start(s8[12582912]{0:T(1024)(128)(4,1)} %bitcast.90), calls=%async_computation.8 | async-start | bytes 8388608
  139.5 5.4 slice-start.2
  144.9 5.4 copy-start.2
  156.0 5.4 copy-start.3
  156.0 22.4 %copy-start.16 = (s32[768]{0:T(1024)S(1)}, s32[768]{0:T(1024)}, u32[]{:S(2)}) copy-start(s32[768]{0:T(1024)} %param.7) | copy-start | bytes 9220
  178.6 14.8 %slice-start.3 = ((s8[12582912]{0:T(1024)(128)(4,1)}), s8[4194304]{0:T(1024)(128)(4,1)S(1)}, s32[]{:S(2)}) async-start(s8[12582912]{0:T(1024)(128)(4,1)} %bitcast.92), calls=%async_computation.10 | async-start | bytes 8388608
  178.6 14.8 %slice-start.4 = ((s8[12582912]{0:T(1024)(128)(4,1)}), s8[4194304]{0:T(1024)(128)(4,1)S(1)}, s32[]{:S(2)}) async-start(s8[12582912]{0:T(1024)(128)(4,1)} %bitcast.92), calls=%async_computation.11 | async-start | bytes 8388608
  184.6 8.7 %copy-start.8 = (bf16[768,1024]{1,0:T(8,128)(2,1)}, bf16[768,1024]{1,0:T(8,128)(2,1)S(1)}, u32[]{:S(2)}) copy-start(bf16[768,1024]{1,0:T(8,128)(2,1)S(1)} %get-tuple-element.30) | copy-start | bytes 4718596
  184.6 8.7 %copy-start.10 = (bf16[768,1024]{1,0:T(8,128)(2,1)}, bf16[768,1024]{1,0:T(8,128)(2,1)S(1)}, u32[]{:S(2)}) copy-start(bf16[768,1024]{1,0:T(8,128)(2,1)S(1)} %get-tuple-element.31) | copy-start | bytes 4718596
  184.6 8.7 %slice-start.5 = ((s8[12582912]{0:T(1024)(128)(4,1)}), s8[4194304]{0:T(1024)(128)(4,1)S(1)}, s32[]{:S(2)}) async-start(s8[12582912]{0:T(1024)(128)(4,1)} %bitcast.92), calls=%async_computation.12 | async-start | bytes 8388608
  193.4 5.4 copy-start.5
  200.0 1.1 copy-start.12
  209.3 269.3 %reduce-scatter.6.cloned.1.call-start = ((), (), s32[]{:S(2)}) async-start(), calls=%async_computation.5 | async-start | bytes 28311552 | tf_op jit(solution)/shard_map/reduce_scatter | solution.py:87
  209.6 6.1 copy-start.11
  209.6 6.1 copy-start.18
  215.7 3.6 copy-start.9
  231.5 407.2 %reduce-scatter.8.cloned.1.call-start = ((), (), s32[]{:S(2)}) async-start(), calls=%async_computation.6 | async-start | bytes 28311552 | tf_op jit(solution)/shard_map/reduce_scatter | solution.py:88
  231.8 6.6 %copy-start.4 = (f32[768,1024]{1,0:T(8,128)S(1)}, f32[768,1024]{1,0:T(8,128)}, u32[]{:S(2)}) copy-start(f32[768,1024]{1,0:T(8,128)} %copy-done.3) | copy-start | bytes 9437188
  231.8 6.6 %copy-start.7 = (bf16[768,4,512]{0,2,1:T(8,128)(2,1)S(1)}, bf16[768,4,512]{0,2,1:T(8,128)(2,1)}, u32[]{:S(2)}) copy-start(bf16[768,4,512]{0,2,1:T(8,128)(2,1)} %copy.12) | copy-start | bytes 9437188
  254.2 1.1 copy-start.1
Sparse Core Ops, SparseCore 0:
  9.6 89.7 all-gather.1
  209.5 108.9 reduce-scatter.3
  322.1 156.5 reduce-scatter.5
  482.7 155.9 reduce-scatter.7
